TPU v7x, 32 devices: a whole 2x2x4 slice. The times are simulated.
32 devices in a mesh: dp: 8 (over z, x), mix: 4 (over y, core).
Axes of the slice: x: 2, y: 2, z: 4, core: 2. Of those that a mesh axis runs over, the one named last changes fastest.
Arguments:
- inputs: bfloat16 [40, 1280, 768], P('dp', 'mix'), may hold values from -6 to 6
- pass_count: int32 [40], P('dp'), may hold values from 2 to 5
- pass_embed: bfloat16 [5, 768], replicated, may hold values from -3 to 3
- ln1_gain: bfloat16 [768], replicated, may hold values from 0.5 to 1.5
- ln1_bias: bfloat16 [768], replicated, may hold values from -0.59765625 to 0.59765625
- w_qkv: bfloat16 [768, 2304], replicated, may hold values from -0.21875 to 0.21875
- bias_q: bfloat16 [768], replicated, may hold values from -0.59765625 to 0.59765625
- bias_v: bfloat16 [768], replicated, may hold values from -0.29882812 to 0.29882812
- w_out: bfloat16 [768, 768], replicated, may hold values from -3.5 to 3.5
- bias_out: bfloat16 [768], replicated, may hold values from -0.59765625 to 0.59765625
- ln2_gain: bfloat16 [768], replicated, may hold values from 0.5 to 1.5
- ln2_bias: bfloat16 [768], replicated, may hold values from -0.59765625 to 0.59765625
- w_up: bfloat16 [768, 3072], replicated, may hold values from -0.21875 to 0.21875
- bias_up: bfloat16 [3072], replicated, may hold values from -0.59765625 to 0.59765625
- w_down: bfloat16 [3072, 768], replicated, may hold values from -0.21875 to 0.21875
- bias_down: bfloat16 [768], replicated, may hold values from -0.59765625 to 0.59765625
- cotangent: bfloat16 [40, 1280, 768], P('dp', 'mix'), may hold values from -6 to 6
Outputs:
- out: float32 [40, 1280, 768], P('dp', 'mix')
- grad_x: float32 [40, 1280, 768], P('dp', 'mix')
- grad_pass_embed: float32 [5, 768], replicated
- grad_ln1_gain: float32 [768], replicated
- grad_ln1_bias: float32 [768], replicated
- grad_w_qkv: float32 [768, 2304], P('dp', 'mix')
- grad_bias_q: float32 [768], replicated
- grad_bias_v: float32 [768], replicated
- grad_w_out: float32 [768, 768], P('dp', 'mix')
- grad_bias_out: float32 [768], replicated
- grad_ln2_gain: float32 [768], replicated
- grad_ln2_bias: float32 [768], replicated
- grad_w_up: float32 [768, 3072], P('dp', 'mix')
- grad_bias_up: float32 [3072], replicated
- grad_w_down: float32 [3072, 768], P('dp', 'mix')
- grad_bias_down: float32 [768], replicated
Inputs may be any that keep to these rules, and one draw needn't show every extreme that they name: Item i uses passes 0 to pass_count[i] - 1 of each token; the other slots are masked.
All inputs are finite; a program needn't handle non-finite values.
Results may differ from a plain program's by a relative error of at most 0.0095.
Values may be sent and summed in bfloat16 or wider, within the bound.
No kernel may reach another device: no remote copies, remote signals or barrier semaphores. Data moves between devices by JAX's collectives and lax.ppermute only.
A program may use at most 256 MiB of HBM per device.

v0:
```python
from functools import partial
import math
import jax
import jax.numpy as jnp
from jax import lax
from jax.sharding import PartitionSpec as P

HEAD = 64
PASSES = 5
epsilon = 1e-05
highest = lax.Precision.HIGHEST


def norm_forward(values, gain_vec, shift_vec):
    center = values - jnp.mean(values, axis=-1, keepdims=True)
    inverse = lax.rsqrt(jnp.mean(center * center, axis=-1, keepdims=True) + epsilon)
    normed = center * inverse
    return (normed * gain_vec + shift_vec, normed, inverse)


def norm_backward(upstream, normed, inverse, gain_vec):
    scaled = upstream * gain_vec
    inner_term = scaled - jnp.mean(scaled, axis=-1, keepdims=True)
    inner_term = inner_term - normed * jnp.mean(scaled * normed, axis=-1, keepdims=True)
    return (inverse * inner_term, jnp.sum(upstream * normed, axis=0), jnp.sum(upstream, axis=0))


def split_parts(stacked):
    slot_total = stacked.shape[0]
    heads_dev = stacked.shape[-1] // HEAD
    queries = stacked[:, 0].reshape(slot_total, heads_dev, HEAD)
    key_rows = stacked[:, 1].reshape(slot_total, heads_dev, HEAD)
    value_rows = stacked[:, 2].reshape(slot_total, heads_dev, HEAD)
    return (queries, key_rows, value_rows)


def score_table(queries, key_rows, passes_item):
    slot_total = key_rows.shape[0]
    raw_scores = jnp.einsum("qhd,khd->hqk", queries, key_rows, preferred_element_type=jnp.float32)
    raw_scores = raw_scores * (1.0 / math.sqrt(HEAD))
    slot_ids = lax.iota(jnp.int32, slot_total)
    allowed = (slot_ids[None, :] <= slot_ids[:, None]) & (slot_ids[None, :] % PASSES < passes_item)
    return jnp.where(allowed[None], raw_scores, -1e30)


def attend_item(pieces):
    stacked, passes_item = pieces
    queries, key_rows, value_rows = split_parts(stacked)
    scores = score_table(queries, key_rows, passes_item)
    row_max = jnp.max(scores, axis=-1, keepdims=True)
    log_total = row_max + jnp.log(jnp.sum(jnp.exp(scores - row_max), axis=-1, keepdims=True))
    weights_low = jnp.exp(scores - log_total).astype(jnp.bfloat16)
    attended = jnp.einsum(
        "hqk,khd->qhd", weights_low, value_rows, preferred_element_type=jnp.float32
    )
    return (attended.reshape(stacked.shape[0], -1).astype(jnp.bfloat16), log_total)


def attend_back(pieces):
    stacked, grad_heads, log_total, passes_item = pieces
    queries, key_rows, value_rows = split_parts(stacked)
    slot_total = stacked.shape[0]
    scores = score_table(queries, key_rows, passes_item)
    probs = jnp.exp(scores - log_total)
    grad_part = grad_heads.reshape(slot_total, -1, HEAD)
    grad_probs = jnp.einsum(
        "qhd,khd->hqk", grad_part, value_rows, preferred_element_type=jnp.float32
    )
    row_inner = jnp.sum(probs * grad_probs, axis=-1, keepdims=True)
    grad_scores = (probs * (grad_probs - row_inner)).astype(jnp.bfloat16)
    score_scale = 1.0 / math.sqrt(HEAD)
    grad_query = (
        jnp.einsum("hqk,khd->qhd", grad_scores, key_rows, preferred_element_type=jnp.float32)
        * score_scale
    )
    grad_key = (
        jnp.einsum("hqk,qhd->khd", grad_scores, queries, preferred_element_type=jnp.float32)
        * score_scale
    )
    grad_value = jnp.einsum(
        "hqk,qhd->khd", probs.astype(jnp.bfloat16), grad_part, preferred_element_type=jnp.float32
    )
    joined = jnp.stack([grad_query, grad_key, grad_value], axis=1).astype(jnp.bfloat16)
    return joined.reshape(slot_total, 3, -1)


def per_device(
    inputs,
    pass_count,
    pass_embed,
    ln1_gain,
    ln1_bias,
    w_qkv,
    bias_q,
    bias_v,
    w_out,
    bias_out,
    ln2_gain,
    ln2_bias,
    w_up,
    bias_up,
    w_down,
    bias_down,
    cotangent,
):
    item_dev, slot_dev, model_width = inputs.shape
    row_total = item_dev * slot_dev
    slot_ids = lax.axis_index("mix") * slot_dev + lax.iota(jnp.int32, slot_dev)
    pass_ids = slot_ids % PASSES
    onehot = (pass_ids[:, None] == lax.iota(jnp.int32, PASSES)[None, :]).astype(jnp.float32)
    keep_mask = (pass_ids[None, :] < pass_count[:, None]).astype(jnp.float32).reshape(row_total, 1)
    pass_rows = jnp.dot(onehot, pass_embed.astype(jnp.float32), precision=highest)
    hidden = (inputs.astype(jnp.float32) + pass_rows[None]).reshape(row_total, model_width)
    gain_one = ln1_gain.astype(jnp.float32)
    gain_two = ln2_gain.astype(jnp.float32)
    first, normed_one, inverse_one = norm_forward(hidden, gain_one, ln1_bias.astype(jnp.float32))
    first_low = first.astype(jnp.bfloat16)
    joined_bias = jnp.concatenate(
        [
            bias_q.astype(jnp.float32),
            jnp.zeros((model_width,), jnp.float32),
            bias_v.astype(jnp.float32),
        ]
    )
    joined = jnp.dot(first_low, w_qkv, preferred_element_type=jnp.float32) + joined_bias
    head_block = lax.all_to_all(
        joined.astype(jnp.bfloat16).reshape(item_dev, slot_dev, 3, model_width),
        "mix",
        split_axis=3,
        concat_axis=1,
        tiled=True,
    )
    attended_heads, log_totals = lax.map(attend_item, (head_block, pass_count))
    attended = lax.all_to_all(
        attended_heads, "mix", split_axis=1, concat_axis=2, tiled=True
    ).reshape(row_total, model_width)
    attn_out = jnp.dot(attended, w_out, preferred_element_type=jnp.float32) + bias_out.astype(
        jnp.float32
    )
    mixed_rows = hidden + keep_mask * attn_out
    second, normed_two, inverse_two = norm_forward(
        mixed_rows, gain_two, ln2_bias.astype(jnp.float32)
    )
    second_low = second.astype(jnp.bfloat16)
    pre_act = jnp.dot(second_low, w_up, preferred_element_type=jnp.float32) + bias_up.astype(
        jnp.float32
    )
    act_low = jax.nn.gelu(pre_act, approximate=True).astype(jnp.bfloat16)
    result = mixed_rows + keep_mask * (
        jnp.dot(act_low, w_down, preferred_element_type=jnp.float32) + bias_down.astype(jnp.float32)
    )
    grad_top = cotangent.astype(jnp.float32).reshape(row_total, model_width)
    grad_mlp = (keep_mask * grad_top).astype(jnp.bfloat16)
    grad_wdown = jnp.dot(act_low.T, grad_mlp, preferred_element_type=jnp.float32)
    grad_bdown = jnp.sum(grad_mlp, axis=0, dtype=jnp.float32)
    unused_out, gelu_back = jax.vjp(partial(jax.nn.gelu, approximate=True), pre_act)
    grad_pre = gelu_back(jnp.dot(grad_mlp, w_down.T, preferred_element_type=jnp.float32))[0].astype(
        jnp.bfloat16
    )
    grad_wup = jnp.dot(second_low.T, grad_pre, preferred_element_type=jnp.float32)
    grad_bup = jnp.sum(grad_pre, axis=0, dtype=jnp.float32)
    grad_norm_two, grad_gain_two, grad_shift_two = norm_backward(
        jnp.dot(grad_pre, w_up.T, preferred_element_type=jnp.float32),
        normed_two,
        inverse_two,
        gain_two,
    )
    grad_mixed = grad_top + grad_norm_two
    grad_attn = (keep_mask * grad_mixed).astype(jnp.bfloat16)
    grad_wout = jnp.dot(attended.T, grad_attn, preferred_element_type=jnp.float32)
    grad_bout = jnp.sum(grad_attn, axis=0, dtype=jnp.float32)
    grad_attended = jnp.dot(grad_attn, w_out.T, preferred_element_type=jnp.float32).astype(
        jnp.bfloat16
    )
    grad_attended = grad_attended.reshape(item_dev, slot_dev, model_width)
    grad_heads = lax.all_to_all(grad_attended, "mix", split_axis=2, concat_axis=1, tiled=True)
    grad_stacked = lax.map(attend_back, (head_block, grad_heads, log_totals, pass_count))
    grad_joined = lax.all_to_all(
        grad_stacked, "mix", split_axis=1, concat_axis=3, tiled=True
    ).reshape(row_total, 3 * model_width)
    grad_wqkv = jnp.dot(first_low.T, grad_joined, preferred_element_type=jnp.float32)
    grad_bq = jnp.sum(grad_joined[:, :model_width], axis=0, dtype=jnp.float32)
    grad_bv = jnp.sum(grad_joined[:, 2 * model_width :], axis=0, dtype=jnp.float32)
    grad_norm_one, grad_gain_one, grad_shift_one = norm_backward(
        jnp.dot(grad_joined, w_qkv.T, preferred_element_type=jnp.float32),
        normed_one,
        inverse_one,
        gain_one,
    )
    grad_hidden = grad_mixed + grad_norm_one
    grad_embed = jnp.dot(
        onehot.T,
        jnp.sum(grad_hidden.reshape(item_dev, slot_dev, model_width), axis=0),
        precision=highest,
    )
    partial_sums = (
        lax.psum_scatter(grad_wqkv, "dp", scatter_dimension=0, tiled=True),
        lax.psum_scatter(grad_wout, "dp", scatter_dimension=0, tiled=True),
        lax.psum_scatter(grad_wup, "dp", scatter_dimension=0, tiled=True),
        lax.psum_scatter(grad_wdown, "dp", scatter_dimension=0, tiled=True),
    )
    reduced = (
        lax.psum_scatter(partial_sums[0], "mix", scatter_dimension=1, tiled=True),
        lax.psum_scatter(partial_sums[1], "mix", scatter_dimension=1, tiled=True),
        lax.psum_scatter(partial_sums[2], "mix", scatter_dimension=1, tiled=True),
        lax.psum_scatter(partial_sums[3], "mix", scatter_dimension=1, tiled=True),
    )
    smalls = lax.psum(
        (
            grad_embed,
            grad_gain_one,
            grad_shift_one,
            grad_bq,
            grad_bv,
            grad_bout,
            grad_gain_two,
            grad_shift_two,
            grad_bup,
            grad_bdown,
        ),
        ("dp", "mix"),
    )
    return (
        result.reshape(item_dev, slot_dev, model_width),
        grad_hidden.reshape(item_dev, slot_dev, model_width),
        smalls[0],
        smalls[1],
        smalls[2],
        reduced[0],
        smalls[3],
        smalls[4],
        reduced[1],
        smalls[5],
        smalls[6],
        smalls[7],
        reduced[2],
        smalls[8],
        reduced[3],
        smalls[9],
    )


def solution(mesh):
    return jax.shard_map(
        per_device,
        mesh=mesh,
        in_specs=(
            P("dp", "mix", None),
            P("dp"),
            P(),
            P(),
            P(),
            P(),
            P(),
            P(),
            P(),
            P(),
            P(),
            P(),
            P(),
            P(),
            P(),
            P(),
            P("dp", "mix", None),
        ),
        out_specs=(
            P("dp", "mix", None),
            P("dp", "mix", None),
            P(),
            P(),
            P(),
            P("dp", "mix"),
            P(),
            P(),
            P("dp", "mix"),
            P(),
            P(),
            P(),
            P("dp", "mix"),
            P(),
            P("dp", "mix"),
            P(),
        ),
        check_vma=False,
    )
```

profile of v0, /device:TPU:0, one launch (start us, length us, event | category | flops | bytes accessed | tf_op | source)
XLA Modules:
  0.0 1744.5 jit_solution(5274464120580839720)
XLA Ops:
  31.3 8.5 add_convert_fusion
  39.8 16.9 reshape.398
  56.7 23.4 %copy.79 = bf16[5,320,3,768]{1,2,0,3:T(4,128)(2,1)} copy(bf16[5,320,3,768]{3,2,1,0:T(4,128)(2,1)} %reshape.398) | data formatting | bytes 14745600 | tf_op jit(solution)/shard_map/reshape | solution.py:127
  86.3 130.4 %all-to-all-done = bf16[5,320,3,768]{1,2,0,3:T(4,128)(2,1)} async-done(((bf16[5,320,3,768]{1,2,0,3:T(4,128)(2,1)}), bf16[5,320,3,768]{1,2,0,3:T(4,128)(2,1)}, u32[]{:S(2)}, u32[]{:S(2)}) %all-to-all-start) | async-done | bytes 7372832 | tf_op jit(solution)/shard_map/all_to_all | solution.py:126
  216.7 9.3 copy.80
  226.0 14.7 copy.81
  240.7 14.7 all_to_all.51
  255.4 182.3 %while.26 = (s32[]{:T(128)}, bf16[5,1280,192]{1,2,0:T(8,128)(2,1)}, f32[5,3,1280,1]{2,1,3,0:T(4,128)}, bf16[5,1280,3,192]{1,3,2,0:T(8,128)(2,1)}, s32[5]{0:T(128)S(1)}, /*index=5*/s32[]{:T(128)}) while((s32[]{:T(128)}, bf16[5,1280,192]{1,2,0:T(8,128)(2,1)}, f32[5,3,1280,1]{2,1,3,0:T(4,128)}, bf16[5,1280,3,192]{1,3,2,0:T(8,128)(2,1)}, ...), condition=%wide.region_5.6_spmd, body=%wide.region_2.5_spmd.sunk | while | flops 1296225280 | bytes 71247464 | solution.py:133
  260.9 9.3 fusion.115
  270.2 9.8 exponential_reduce_fusion.2
  281.4 9.9 fusion.116
  297.3 9.3 fusion.115
  306.7 9.8 exponential_reduce_fusion.2
  317.8 9.9 fusion.116
  333.8 9.3 fusion.115
  343.1 9.8 exponential_reduce_fusion.2
  354.2 9.9 fusion.116
  370.2 9.3 fusion.115
  379.5 9.8 exponential_reduce_fusion.2
  390.6 9.9 fusion.116
  406.6 9.3 fusion.115
  415.9 9.8 exponential_reduce_fusion.2
  427.0 9.9 fusion.116
  437.7 7.4 copy.82
  465.4 21.5 %all-to-all-done.1 = bf16[4,2,153600]{2,1,0:T(2,128)(2,1)} async-done(((bf16[4,2,153600]{2,1,0:T(2,128)(2,1)}), bf16[4,2,153600]{2,1,0:T(2,128)(2,1)}, u32[]{:S(2)}, u32[]{:S(2)}) %all-to-all-start.1) | async-done | bytes 2457632 | tf_op jit(solution)/shard_map/all_to_all | solution.py:134
  514.5 19.6 %multiply_convert_fusion.1 = (bf16[1600,3072]{1,0:T(8,128)(2,1)}, f32[1600,3072]{1,0:T(8,128)}) fusion(f32[3072]{0:T(1024)S(1)} %copy-done.29, bf16[768,3072]{1,0:T(8,128)(2,1)} %param.33, f32[1600,768]{1,0:T(8,128)S(1)} %get-tuple-element.304, f32[768]{0:T(1024)S(1)} %copy-done.30, f32[768]{0:T(1024)S(1)} %copy-done.28, f32[1600]{0:T(1024)S(1)} %add_rsqrt_fusion.1, ...), kind=kOutput, calls=%fused_computation.53 | convolution fusion | flops 7605043200 | bytes 39156224 | tf_op jit(solution)/shard_map/dot_general | solution.py:145
  534.0 24.4 %convert_reduce_fusion = (f32[3072]{0:T(1024)}, bf16[1600,3072]{1,0:T(8,128)(2,1)}) fusion(f32[1600,3072]{1,0:T(8,128)} %get-tuple-element.306, f32[3072]{0:T(1024)S(1)} %copy-done.29, bf16[1600,768]{1,0:T(8,128)(2,1)S(1)} %copy-done.7, bf16[3072,768]{1,0:T(8,128)(2,1)} %param.35), kind=kOutput, calls=%fused_computation.52 | convolution fusion | flops 7662793728 | bytes 36691968 | tf_op jit(solution)/shard_map/dot_general | solution.py:157
  558.5 15.0 multiply_reduce_fusion.1
  593.9 53.8 %all-to-all-done.2 = bf16[5,320,768]{1,0,2:T(8,128)(2,1)} async-done(((bf16[5,320,768]{1,0,2:T(8,128)(2,1)}), bf16[5,320,768]{1,0,2:T(8,128)(2,1)}, u32[]{:S(2)}, u32[]{:S(2)}) %all-to-all-start.2) | async-done | bytes 2457632 | tf_op jit(solution)/shard_map/all_to_all | solution.py:176
  660.1 286.4 %while.27 = (s32[]{:T(128)}, bf16[5,1280,3,192]{1,3,2,0:T(8,128)(2,1)}, bf16[5,1280,3,192]{1,3,2,0:T(8,128)(2,1)}, s32[5]{0:T(128)S(1)}, f32[5,3,1280,1]{2,1,3,0...) while((s32[]{:T(128)}, bf16[5,1280,3,192]{1,3,2,0:T(8,128)(2,1)}, ...), condition=%wide.region_12.13_spmd, body=%wide.region_10.12_spmd.sunk | while | flops 3198899200 | bytes 167523984 | solution.py:177
  666.4 8.7 fusion.129
  675.1 10.5 fusion.130
  685.6 12.3 multiply_reduce_fusion.10
  698.0 13.2 multiply_convert_fusion.5
  723.7 8.7 fusion.129
  732.4 10.5 fusion.130
  742.9 12.3 multiply_reduce_fusion.10
  755.2 13.2 multiply_convert_fusion.5
  781.0 8.7 fusion.129
  789.7 10.5 fusion.130
  800.2 12.3 multiply_reduce_fusion.10
  812.5 13.2 multiply_convert_fusion.5
  838.2 8.7 fusion.129
  846.9 10.5 fusion.130
  857.4 12.3 multiply_reduce_fusion.10
  869.8 13.2 multiply_convert_fusion.5
  895.5 8.7 fusion.129
  904.2 10.5 fusion.130
  914.7 12.3 multiply_reduce_fusion.10
  927.0 13.2 multiply_convert_fusion.5
  946.5 19.2 %copy.87 = bf16[5,1280,3,192]{3,2,0,1:T(4,128)(2,1)} copy(bf16[5,1280,3,192]{1,3,2,0:T(8,128)(2,1)} %get-tuple-element.163) | data formatting | bytes 14745600 | tf_op jit(solution)/shard_map/while | solution.py:177
  978.6 137.2 %all-to-all-done.3 = bf16[5,1280,3,192]{3,2,0,1:T(4,128)(2,1)} async-done(((bf16[5,1280,3,192]{3,2,0,1:T(4,128)(2,1)}), bf16[5,1280,3,192]{3,2,0,1:T(4,128)(2,1)}, u32[]{:S(2)}, u32[]{:S(2)}) %all-to-all-start.3) | async-done | bytes 7372832 | tf_op jit(solution)/shard_map/all_to_all | solution.py:178
  1115.8 24.6 %copy.103 = bf16[5,4,320,3,192]{4,1,3,2,0:T(4,128)(2,1)} copy(bf16[5,4,320,3,192]{4,3,0,2,1:T(4,128)(2,1)} %bitcast.32) | data formatting | bytes 14745600 | tf_op jit(solution)/shard_map/all_to_all | solution.py:178
  1140.4 16.9 reshape.403
  1157.3 12.1 fusion.47
  1169.7 14.4 fusion.49
  1186.2 16.1 fusion.41
  1202.4 97.4 %reduce-scatter.15.cloned.1.call-done = f32[96,2304]{1,0:T(8,128)} async-done(((f32[768,2304]{1,0:T(8,128)}), f32[96,2304]{1,0:T(8,128)}) %reduce-scatter.15.cloned.1.call-update) | async-done | bytes 884752 | tf_op jit(solution)/shard_map/reduce_scatter | solution.py:197
  1302.5 162.2 %reduce-scatter.23.cloned.1.call-done = f32[384,768]{1,0:T(8,128)} async-done(((f32[3072,768]{1,0:T(8,128)}), f32[384,768]{1,0:T(8,128)}) %reduce-scatter.23.cloned.1.call-update) | async-done | bytes 1179664 | tf_op jit(solution)/shard_map/reduce_scatter | solution.py:200
  1470.4 14.4 multiply_add_fusion.1
  1488.6 164.0 %reduce-scatter.19.cloned.1.call-done = f32[96,3072]{1,0:T(8,128)} async-done(((f32[768,3072]{1,0:T(8,128)}), f32[96,3072]{1,0:T(8,128)}) %reduce-scatter.19.cloned.1.call-update) | async-done | bytes 1179664 | tf_op jit(solution)/shard_map/reduce_scatter | solution.py:199
  1652.6 14.2 multiply_reduce_fusion.2
  1682.4 41.3 %all-reduce = (f32[5,768]{1,0:T(8,128)}, f32[768]{0:T(1024)}, f32[768]{0:T(1024)}, f32[768]{0:T(1024)}, f32[768]{0:T(1024)}, /*index=5*/f32[768]{0:T(1024)}, f32...) all-reduce(f32[5,768]{1,0:T(8,128)} %fusion.34, ...), channel_id=1, replica_groups=mesh['dp'=8,'mix'=4] {'dp','mix'}, use_global_device_ids=true, to_apply=%region_16.17 | all-reduce | flops 13056 | bytes 104448 | tf_op jit(solution)/shard_map/psum | solution.py:208
  1725.6 11.7 reduce-scatter.21.cloned.1.call-done
  (246 shorter events, 255.1 us)
Async XLA Ops:
  7.2 24.1 %copy-start = (bf16[768,2304]{1,0:T(8,128)(2,1)S(1)}, bf16[768,2304]{1,0:T(8,128)(2,1)}, u32[]{:S(2)}) copy-start(bf16[768,2304]{1,0:T(8,128)(2,1)} %param.26) | copy-start | bytes 10616836
  7.2 0.6 copy-start.21
  9.1 0.9 copy-start.5
  16.8 12.4 copy-start.13
  22.6 6.5 copy-start.25
  22.6 6.5 copy-start.26
  22.6 8.7 copy-start.15
  22.6 8.7 copy-start.17
  22.6 8.7 copy-start.24
  29.1 2.2 copy-start.3
  80.1 136.6 %all-to-all-start = ((bf16[5,320,3,768]{1,2,0,3:T(4,128)(2,1)}), bf16[5,320,3,768]{1,2,0,3:T(4,128)(2,1)}, u32[]{:S(2)}, u32[]{:S(2)}) async-start(bf16[5,320,3,768]{1,2,0,3:T(4,128)(2,1)} %copy.79), calls=%async_computation | async-start | bytes 23592960 | tf_op jit(solution)/shard_map/all_to_all | solution.py:126
  240.7 14.8 copy-start.35
  445.1 12.1 copy-start.32
  445.1 12.7 copy-start.33
  445.1 13.3 copy-start.34
  445.1 13.9 copy-start.22
  452.3 34.5 %all-to-all-start.1 = ((bf16[4,2,153600]{2,1,0:T(2,128)(2,1)}), bf16[4,2,153600]{2,1,0:T(2,128)(2,1)}, u32[]{:S(2)}, u32[]{:S(2)}) async-start(bf16[4,2,153600]{2,1,0:T(2,128)(2,1)} %reshape.412), calls=%async_computation.1 | async-start | bytes 4915200 | tf_op jit(solution)/shard_map/all_to_all | solution.py:134
  459.8 34.3 %copy-start.8 = (f32[5,320]{1,0:T(8,128)}, f32[5,320]{1,0:T(8,128)S(1)}, u32[]{:S(2)}) copy-start(f32[5,320]{1,0:T(8,128)S(1)} %compare_convert_fusion) | copy-start | bytes 19204
  501.1 6.6 copy-start.10
  501.1 6.6 copy-start.31
  513.7 59.8 %copy-start.4 = (f32[1600,768]{1,0:T(8,128)}, f32[1600,768]{1,0:T(8,128)S(1)}, u32[]{:S(2)}) copy-start(f32[1600,768]{1,0:T(8,128)S(1)} %get-tuple-element.304) | copy-start | bytes 14745604
  513.7 0.7 copy-start.28
  513.7 0.8 copy-start.29
  513.7 0.8 copy-start.30
  513.7 59.8 %copy-start.11 = (f32[1600]{0:T(1024)}, f32[1600]{0:T(1024)S(1)}, u32[]{:S(2)}) copy-start(f32[1600]{0:T(1024)S(1)} %broadcast_multiply_fusion.5) | copy-start | bytes 19204
  514.5 59.0 %copy-start.19 = (f32[1600]{0:T(1024)}, f32[1600]{0:T(1024)S(1)}, u32[]{:S(2)}) copy-start(f32[1600]{0:T(1024)S(1)} %add_rsqrt_fusion.1) | copy-start | bytes 19204
  514.5 19.6 %copy-start.7 = (bf16[1600,768]{1,0:T(8,128)(2,1)S(1)}, bf16[1600,768]{1,0:T(8,128)(2,1)}, u32[]{:S(2)}) copy-start(bf16[1600,768]{1,0:T(8,128)(2,1)} %fusion.28) | copy-start | bytes 7372804
  558.5 15.0 copy-start.2
  573.5 5.4 copy-start.37
  578.9 3.6 copy-start.6
  588.9 58.8 %all-to-all-start.2 = ((bf16[5,320,768]{1,0,2:T(8,128)(2,1)}), bf16[5,320,768]{1,0,2:T(8,128)(2,1)}, u32[]{:S(2)}, u32[]{:S(2)}) async-start(bf16[5,320,768]{1,0,2:T(8,128)(2,1)} %copy.84), calls=%async_computation.2 | async-start | bytes 9437184 | tf_op jit(solution)/shard_map/all_to_all | solution.py:176
  647.7 12.4 copy-start.36
  713.0 3.1 copy-start.1
  770.3 3.1 copy-start.1
  827.6 3.1 copy-start.1
  884.8 3.1 copy-start.1
  942.1 3.1 copy-start.1
  965.7 150.1 %all-to-all-start.3 = ((bf16[5,1280,3,192]{3,2,0,1:T(4,128)(2,1)}), bf16[5,1280,3,192]{3,2,0,1:T(4,128)(2,1)}, u32[]{:S(2)}, u32[]{:S(2)}) async-start(bf16[5,1280,3,192]{3,2,0,1:T(4,128)(2,1)} %copy.87), calls=%async_computation.3 | async-start | bytes 26214400 | tf_op jit(solution)/shard_map/all_to_all | solution.py:178
  972.1 212.1 %reduce-scatter.17.cloned.1.call-start = ((), (), s32[]{:S(2)}) async-start(), calls=%async_computation.13 | async-start | bytes 2654208 | tf_op jit(solution)/shard_map/reduce_scatter | solution.py:198
  978.5 321.3 %reduce-scatter.15.cloned.1.call-start = ((), (), s32[]{:S(2)}) async-start(), calls=%async_computation.12 | async-start | bytes 7962624 | tf_op jit(solution)/shard_map/reduce_scatter | solution.py:197
  1169.5 295.2 %reduce-scatter.23.cloned.1.call-start = ((), (), s32[]{:S(2)}) async-start(), calls=%async_computation.16 | async-start | bytes 10616832 | tf_op jit(solution)/shard_map/reduce_scatter | solution.py:200
  1184.1 2.1 copy-start.12
  1184.1 2.1 copy-start.20
  1184.2 302.8 %reduce-scatter.27.cloned.1.call-start = ((), (), s32[]{:S(2)}) async-start(), calls=%async_computation.18 | async-start | bytes 491520
  1186.1 466.4 %reduce-scatter.19.cloned.1.call-start = ((), (), s32[]{:S(2)}) async-start(), calls=%async_computation.14 | async-start | bytes 10616832 | tf_op jit(solution)/shard_map/reduce_scatter | solution.py:199
  1202.3 265.1 %copy-start.9 = (f32[5,320]{1,0:T(8,128)S(1)}, f32[5,320]{1,0:T(8,128)}, u32[]{:S(2)}) copy-start(f32[5,320]{1,0:T(8,128)} %copy-done.8) | copy-start | bytes 19204
  1202.4 521.4 %reduce-scatter.25.cloned.1.call-start = ((), (), s32[]{:S(2)}) async-start(), calls=%async_computation.17 | async-start | bytes 1474560
  1302.4 423.1 %reduce-scatter.29.cloned.1.call-start = ((), (), s32[]{:S(2)}) async-start(), calls=%async_computation.19 | async-start | bytes 1474560
  1467.4 269.9 %reduce-scatter.21.cloned.1.call-start = ((), (), s32[]{:S(2)}) async-start(), calls=%async_computation.15 | async-start | bytes 1474560 | tf_op jit(solution)/shard_map/reduce_scatter | solution.py:205
  1470.4 182.2 %copy-start.14 = (f32[768]{0:T(1024)S(1)}, f32[768]{0:T(1024)}, u32[]{:S(2)}) copy-start(f32[768]{0:T(1024)} %copy-done.13) | copy-start | bytes 9220
  1470.4 182.2 %copy-start.16 = (f32[1600]{0:T(1024)S(1)}, f32[1600]{0:T(1024)}, u32[]{:S(2)}) copy-start(f32[1600]{0:T(1024)} %div.27) | copy-start | bytes 19204
  1652.6 14.2 copy-start.18
  1673.1 3.8 copy-start.23
  1673.1 9.3 copy-start.27
Sparse Core Ops, SparseCore 0:
  978.7 71.9 reduce-scatter.16
  1169.6 130.1 reduce-scatter.14
  1303.4 161.2 reduce-scatter.22
  1467.0 19.8 reduce-scatter.26
  1490.4 162.0 reduce-scatter.18
  1654.9 24.7 reduce-scatter.24
  1682.8 25.6 reduce-scatter.28
  1711.6 25.5 reduce-scatter.20
where the time goes:
time: 1760 us; the launch traced here: 1740 us
  waiting for transfers between devices  780 us (44%)
  matrix products  436 us (25%)
  local copies, waits for them, and re-layouts  250 us (14%)
  other arithmetic  198 us (11%)
  blocking collectives  41.3 us (2%)
  starting transfers between devices  23.2 us (1%)
    reduce_scatter x1, waiting for transfers between devices, per_device(): lax.psum_scatter(grad_wup, 'dp', scatter_dimension=0, tiled=True)  164 us
    reduce_scatter x1, waiting for transfers between devices, per_device(): lax.psum_scatter(grad_wdown, 'dp', scatter_dimension=0, tiled=True)  162 us
    all_to_all x1, waiting for transfers between devices, per_device(): lax.all_to_all(grad_stacked, 'mix', split_axis=1, concat_axis=3, tiled=True)  137 us
    all_to_all x1, waiting for transfers between devices, per_device(): lax.all_to_all(joined.astype(jnp.bfloat16).reshape(item_dev, slot_dev, 3,...  130 us
    reduce_scatter x1, waiting for transfers between devices, per_device(): lax.psum_scatter(grad_wqkv, 'dp', scatter_dimension=0, tiled=True)  97.4 us
    dot_general x10, matrix products, score_table(): jnp.einsum('qhd,khd->hqk', queries, key_rows, preferred_element_type=jnp....  90 us
    convert_element_type x5, other arithmetic, attend_back(): grad_scores = (probs * (grad_probs - row_inner)).astype(jnp.bfloat16)  66.2 us
    dot_general x5, matrix products, attend_back(): jnp.einsum('qhd,khd->hqk', grad_part, value_rows, preferred_element_type=...  61.7 us
  transfers between devices with their start and end apart: 12, of which 9 were waited for; matrix products, arithmetic and copies ran while one was open for 9% of the time, Pallas kernels for 0%

commit v1 on v0

--- a/solution.py
+++ b/solution.py
@@ -9,6 +9,18 @@
 PASSES = 5
 epsilon = 1e-05
 highest = lax.Precision.HIGHEST
+
+
+def in_blocks(array, dim, count):
+    lengths = array.shape
+    blocks = array.reshape(*lengths[:dim], count, lengths[dim] // count, *lengths[dim + 1 :])
+    return jnp.moveaxis(blocks, dim, 0)
+
+
+def laid_out(parts, dim):
+    shape = list(parts.shape[1:])
+    shape[dim] *= parts.shape[0]
+    return jnp.moveaxis(parts, 0, dim).reshape(shape)
 
 
 def norm_forward(values, gain_vec, shift_vec):
@@ -123,13 +135,15 @@
         ]
     )
     joined = jnp.dot(first_low, w_qkv, preferred_element_type=jnp.float32) + joined_bias
-    head_block = lax.all_to_all(
-        joined.astype(jnp.bfloat16).reshape(item_dev, slot_dev, 3, model_width),
-        "mix",
-        split_axis=3,
-        concat_axis=1,
-        tiled=True,
-    )
+    value = joined.astype(jnp.bfloat16).reshape(item_dev, slot_dev, 3, model_width)
+    length, index = (lax.axis_size("mix"), lax.axis_index("mix"))
+    parts = in_blocks(value, 3, length)
+    done = [parts[index]]
+    for step in range(1, length):
+        sent = parts[index ^ step]
+        done.append(lax.ppermute(sent, "mix", [(i, i ^ step) for i in range(length)]))
+    parts = jnp.stack(done)[index ^ jnp.arange(length)]
+    head_block = laid_out(parts, 1)
     attended_heads, log_totals = lax.map(attend_item, (head_block, pass_count))
     attended = lax.all_to_all(
         attended_heads, "mix", split_axis=1, concat_axis=2, tiled=True

time: 1760 us -> 1790 us (1.017)
  local copies, waits for them, and re-layouts: 250 us -> 317 us
  waiting for transfers between devices: 780 us -> 725 us
  other arithmetic: 198 us -> 217 us
    all_to_all x1 -> x0, waiting for transfers between devices: 130 us -> none  [per_device(): lax.all_to_all(joined.astype(jnp.bfloat16).reshape(item_dev, slot_dev, 3,...]
    another operation x0 -> x6, local copies, waits for them, and re-layouts: none -> 91.9 us
    ppermute x0 -> x3, waiting for transfers between devices: none -> 75.5 us  [per_device(): lax.ppermute(sent, 'mix', [(i, i ^ step) for i in range(length)])]
    all_to_all x3 -> x0, local copies, waits for them, and re-layouts: 38.8 us -> none  [per_device(): lax.all_to_all(joined.astype(jnp.bfloat16).reshape(item_dev, slot_dev, 3,...]
    reshape x2 -> x1, local copies, waits for them, and re-layouts: 40.3 us -> 14.8 us  [laid_out(): return jnp.moveaxis(parts, 0, dim).reshape(shape)]
    gather x0 -> x5, local copies, waits for them, and re-layouts: none -> 24.8 us  [per_device(): parts = jnp.stack(done)[index ^ jnp.arange(length)]]
  transfers between devices with their start and end apart: 12 -> 14, of which waited for: 9 -> 10; matrix products, arithmetic and copies ran while one was open for 9% -> 11% of each run, Pallas kernels for 0% -> 0%
where the time goes in v1:
time: 1790 us; the launch traced here: 1770 us
  waiting for transfers between devices  725 us (41%)
  matrix products  436 us (24%)
  local copies, waits for them, and re-layouts  317 us (18%)
  other arithmetic  217 us (12%)
  blocking collectives  41.3 us (2%)
  starting transfers between devices  19.9 us (1%)
    reduce_scatter x1, waiting for transfers between devices, per_device(): lax.psum_scatter(grad_wup, 'dp', scatter_dimension=0, tiled=True)  164 us
    reduce_scatter x1, waiting for transfers between devices, per_device(): lax.psum_scatter(grad_wdown, 'dp', scatter_dimension=0, tiled=True)  162 us
    all_to_all x1, waiting for transfers between devices, per_device(): lax.all_to_all(grad_stacked, 'mix', split_axis=1, concat_axis=3, tiled=True)  137 us
    reduce_scatter x1, waiting for transfers between devices, per_device(): lax.psum_scatter(grad_wqkv, 'dp', scatter_dimension=0, tiled=True)  96.7 us
    dot_general x10, matrix products, score_table(): jnp.einsum('qhd,khd->hqk', queries, key_rows, preferred_element_type=jnp....  90.2 us
    ppermute x3, waiting for transfers between devices, per_device(): lax.ppermute(sent, 'mix', [(i, i ^ step) for i in range(length)])  75.5 us
    another operation x5, local copies, waits for them, and re-layouts  72.9 us
    convert_element_type x5, other arithmetic, attend_back(): grad_scores = (probs * (grad_probs - row_inner)).astype(jnp.bfloat16)  66.2 us
  transfers between devices with their start and end apart: 14, of which 10 were waited for; matrix products, arithmetic and copies ran while one was open for 11% of the time, Pallas kernels for 0%

profile of v1, /device:TPU:0, one launch (start us, length us, event | category | flops | bytes accessed | tf_op | source)
XLA Modules:
  0.0 1772.1 jit_solution(5453899505522165566)
XLA Ops:
  39.8 19.0 %reshape_reshape.3 = bf16[5,320,3,4,192]{4,3,2,1,0:T(4,128)(2,1)} reshape(bf16[1600,2304]{1,0:T(8,128)(2,1)} %add_convert_fusion) | data formatting | bytes 14745600 | tf_op jit(solution)/shard_map/reshape;reshape | solution.py:16
  58.8 31.7 %constant_dynamic-slice_fusion.4 = (bf16[5,320,3,1,192]{4,3,2,1,0:T(2,128)(2,1)}, bf16[5,320,3,1,192]{4,3,2,1,0:T(2,128)(2,1)}, bf16[5,320,3,1,192]{4,3,2,1,0:T(2,128)(2,1)}, bf16[5,320,3,1,192]{4,3,2,1,0:T(2,128)(2,1)}) fusion(bf16[5,320,3,4,192]{4,3,2,1,0:T(4,128)(2,1)} %reshape_reshape.3, s32[]{:T(128)S(6)} %select_n.81, s32[]{:T(128)S(6)} %select_n.84, ...), kind=kLoop, calls=%fused_computation.120 | loop fusion | bytes 14745616 | tf_op jit(solution)/shard_map/dynamic-slice
  90.5 10.3 copy.74
  101.3 10.3 copy.75
  114.0 10.3 copy.76
  124.5 10.3 copy.73
  134.8 28.5 %collective-permute-done.1 = bf16[5,320,3,192]{1,3,2,0:T(8,128)(2,1)} collective-permute-done((bf16[5,320,3,192]{1,3,2,0:T(8,128)(2,1)}, bf16[5,320,3,192]{1,3,2,0:T(8,128)(2,1)}, u32[]{:S(2)}, u32[]{:S(2)}) %collective-permute-start.1) | collective-permute-done | bytes 1843232 | tf_op jit(solution)/shard_map/ppermute | solution.py:144
  163.3 47.0 %collective-permute-done.2 = bf16[5,320,3,192]{1,3,2,0:T(8,128)(2,1)} collective-permute-done((bf16[5,320,3,192]{1,3,2,0:T(8,128)(2,1)}, bf16[5,320,3,192]{1,3,2,0:T(8,128)(2,1)}, u32[]{:S(2)}, u32[]{:S(2)}) %collective-permute-start.2) | collective-permute-done | bytes 1843232 | tf_op jit(solution)/shard_map/ppermute | solution.py:144
  254.6 14.7 copy.79
  269.3 14.8 reshape.421
  284.0 182.2 %while.26 = (s32[]{:T(128)}, bf16[5,1280,192]{1,2,0:T(8,128)(2,1)}, f32[5,3,1280,1]{2,1,3,0:T(4,128)}, bf16[5,1280,3,192]{1,3,2,0:T(8,128)(2,1)}, s32[5]{0:T(128)S(1)}, /*index=5*/s32[]{:T(128)}) while((s32[]{:T(128)}, bf16[5,1280,192]{1,2,0:T(8,128)(2,1)}, f32[5,3,1280,1]{2,1,3,0:T(4,128)}, bf16[5,1280,3,192]{1,3,2,0:T(8,128)(2,1)}, ...), condition=%wide.region_5.6_spmd, body=%wide.region_2.5_spmd.sunk | while | flops 1296225280 | bytes 71247464 | solution.py:147
  289.3 9.3 fusion.116
  298.7 9.8 exponential_reduce_fusion.2
  309.8 9.9 fusion.117
  325.8 9.3 fusion.116
  335.1 9.8 exponential_reduce_fusion.2
  346.2 9.9 fusion.117
  362.2 9.3 fusion.116
  371.6 9.8 exponential_reduce_fusion.2
  382.7 9.9 fusion.117
  398.7 9.3 fusion.116
  408.0 9.8 exponential_reduce_fusion.2
  419.1 9.9 fusion.117
  435.1 9.3 fusion.116
  444.5 9.8 exponential_reduce_fusion.2
  455.6 9.9 fusion.117
  493.6 21.5 %all-to-all-done = bf16[4,2,153600]{2,1,0:T(2,128)(2,1)} async-done(((bf16[4,2,153600]{2,1,0:T(2,128)(2,1)}), bf16[4,2,153600]{2,1,0:T(2,128)(2,1)}, u32[]{:S(2)}, u32[]{:S(2)}) %all-to-all-start) | async-done | bytes 2457632 | tf_op jit(solution)/shard_map/all_to_all | solution.py:148
  542.8 19.6 %multiply_convert_fusion.1 = (bf16[1600,3072]{1,0:T(8,128)(2,1)}, f32[1600,3072]{1,0:T(8,128)}) fusion(f32[3072]{0:T(1024)S(1)} %copy-done.30, bf16[768,3072]{1,0:T(8,128)(2,1)} %param.33, f32[1600,768]{1,0:T(8,128)S(1)} %get-tuple-element.292, f32[768]{0:T(1024)S(1)} %copy-done.31, f32[768]{0:T(1024)S(1)} %copy-done.29, f32[1600]{0:T(1024)S(1)} %add_rsqrt_fusion.1, ...), kind=kOutput, calls=%fused_computation.55 | convolution fusion | flops 7605043200 | bytes 39156224 | tf_op jit(solution)/shard_map/dot_general | solution.py:159
  562.4 24.7 %convert_reduce_fusion = (f32[3072]{0:T(1024)}, bf16[1600,3072]{1,0:T(8,128)(2,1)}) fusion(f32[1600,3072]{1,0:T(8,128)} %get-tuple-element.294, f32[3072]{0:T(1024)S(1)} %copy-done.30, bf16[1600,768]{1,0:T(8,128)(2,1)S(1)} %copy-done.8, bf16[3072,768]{1,0:T(8,128)(2,1)} %param.35), kind=kOutput, calls=%fused_computation.54 | convolution fusion | flops 7662793728 | bytes 36691968 | tf_op jit(solution)/shard_map/dot_general | solution.py:171
  587.0 15.0 multiply_reduce_fusion.1
  622.2 53.8 %all-to-all-done.1 = bf16[5,320,768]{1,0,2:T(8,128)(2,1)} async-done(((bf16[5,320,768]{1,0,2:T(8,128)(2,1)}), bf16[5,320,768]{1,0,2:T(8,128)(2,1)}, u32[]{:S(2)}, u32[]{:S(2)}) %all-to-all-start.1) | async-done | bytes 2457632 | tf_op jit(solution)/shard_map/all_to_all | solution.py:190
  688.4 286.4 %while.27 = (s32[]{:T(128)}, bf16[5,1280,3,192]{1,3,2,0:T(8,128)(2,1)}, bf16[5,1280,3,192]{1,3,2,0:T(8,128)(2,1)}, s32[5]{0:T(128)S(1)}, f32[5,3,1280,1]{2,1,3,0...) while((s32[]{:T(128)}, bf16[5,1280,3,192]{1,3,2,0:T(8,128)(2,1)}, ...), condition=%wide.region_12.13_spmd, body=%wide.region_10.12_spmd.sunk | while | flops 3198899200 | bytes 167523984 | solution.py:191
  694.8 8.7 fusion.130
  703.5 10.5 fusion.131
  714.0 12.3 multiply_reduce_fusion.10
  726.3 13.2 multiply_convert_fusion.5
  760.8 10.5 fusion.131
  771.3 12.3 multiply_reduce_fusion.10
  783.6 13.2 multiply_convert_fusion.5
  818.0 10.5 fusion.131
  828.5 12.3 multiply_reduce_fusion.10
  840.9 13.2 multiply_convert_fusion.5
  866.6 8.7 fusion.130
  875.3 10.5 fusion.131
  885.8 12.3 multiply_reduce_fusion.10
  898.1 13.2 multiply_convert_fusion.5
  923.9 8.7 fusion.130
  932.6 10.5 fusion.131
  943.1 12.3 multiply_reduce_fusion.10
  955.4 13.2 multiply_convert_fusion.5
  974.8 19.3 %copy.85 = bf16[5,1280,3,192]{3,2,0,1:T(4,128)(2,1)} copy(bf16[5,1280,3,192]{1,3,2,0:T(8,128)(2,1)} %get-tuple-element.163) | data formatting | bytes 14745600 | tf_op jit(solution)/shard_map/while | solution.py:191
  1007.2 137.0 %all-to-all-done.2 = bf16[5,1280,3,192]{3,2,0,1:T(4,128)(2,1)} async-done(((bf16[5,1280,3,192]{3,2,0,1:T(4,128)(2,1)}), bf16[5,1280,3,192]{3,2,0,1:T(4,128)(2,1)}, u32[]{:S(2)}, u32[]{:S(2)}) %all-to-all-start.2) | async-done | bytes 7372832 | tf_op jit(solution)/shard_map/all_to_all | solution.py:192
  1144.2 24.6 %copy.101 = bf16[5,4,320,3,192]{4,1,3,2,0:T(4,128)(2,1)} copy(bf16[5,4,320,3,192]{4,3,0,2,1:T(4,128)(2,1)} %bitcast.39) | data formatting | bytes 14745600 | tf_op jit(solution)/shard_map/all_to_all | solution.py:192
  1168.8 16.9 reshape.426
  1185.7 12.2 fusion.48
  1198.1 14.4 fusion.50
  1214.6 16.0 fusion.42
  1230.7 96.7 %reduce-scatter.15.cloned.1.call-done = f32[96,2304]{1,0:T(8,128)} async-done(((f32[768,2304]{1,0:T(8,128)}), f32[96,2304]{1,0:T(8,128)}) %reduce-scatter.15.cloned.1.call-update) | async-done | bytes 884752 | tf_op jit(solution)/shard_map/reduce_scatter | solution.py:211
  1330.1 162.2 %reduce-scatter.23.cloned.1.call-done = f32[384,768]{1,0:T(8,128)} async-done(((f32[3072,768]{1,0:T(8,128)}), f32[384,768]{1,0:T(8,128)}) %reduce-scatter.23.cloned.1.call-update) | async-done | bytes 1179664 | tf_op jit(solution)/shard_map/reduce_scatter | solution.py:214
  1498.0 14.4 multiply_add_fusion.1
  1516.2 163.9 %reduce-scatter.19.cloned.1.call-done = f32[96,3072]{1,0:T(8,128)} async-done(((f32[768,3072]{1,0:T(8,128)}), f32[96,3072]{1,0:T(8,128)}) %reduce-scatter.19.cloned.1.call-update) | async-done | bytes 1179664 | tf_op jit(solution)/shard_map/reduce_scatter | solution.py:213
  1680.2 14.2 multiply_reduce_fusion.2
  1710.0 41.3 %all-reduce = (f32[5,768]{1,0:T(8,128)}, f32[768]{0:T(1024)}, f32[768]{0:T(1024)}, f32[768]{0:T(1024)}, f32[768]{0:T(1024)}, /*index=5*/f32[768]{0:T(1024)}, f32...) all-reduce(f32[5,768]{1,0:T(8,128)} %fusion.34, ...), channel_id=1, replica_groups=mesh['dp'=8,'mix'=4] {'dp','mix'}, use_global_device_ids=true, to_apply=%region_16.17 | all-reduce | flops 13056 | bytes 104448 | tf_op jit(solution)/shard_map/psum | solution.py:222
  1753.2 11.7 reduce-scatter.21.cloned.1.call-done
  (265 shorter events, 329.3 us)
Async XLA Ops:
  7.2 24.1 %copy-start = (bf16[768,2304]{1,0:T(8,128)(2,1)S(1)}, bf16[768,2304]{1,0:T(8,128)(2,1)}, u32[]{:S(2)}) copy-start(bf16[768,2304]{1,0:T(8,128)(2,1)} %param.26) | copy-start | bytes 10616836
  7.2 0.6 copy-start.22
  9.2 0.9 copy-start.6
  16.8 12.3 copy-start.14
  22.6 6.5 copy-start.26
  22.6 6.5 copy-start.27
  22.6 8.7 copy-start.16
  22.6 8.7 copy-start.18
  22.6 8.7 copy-start.25
  29.1 2.2 copy-start.4
  100.8 34.0 %collective-permute-start = (bf16[5,320,3,192]{1,3,2,0:T(8,128)(2,1)}, bf16[5,320,3,192]{1,3,2,0:T(8,128)(2,1)}, u32[]{:S(2)}, u32[]{:S(2)}) collective-permute-start(bf16[5,320,3,192]{1,3,2,0:T(8,128)(2,1)} %bitcast.198), channel_id=1, source_target_pairs={{0,1},{1,0},{2,3},{3,2},{4,5},{5,4},{6,7},{7,6},{8,9},{9,8},{10,11... | collective-permute-start | bytes 5529608 | tf_op jit(solution)/shard_map/ppermute | solution.py:144
  111.5 51.8 %collective-permute-start.1 = (bf16[5,320,3,192]{1,3,2,0:T(8,128)(2,1)}, bf16[5,320,3,192]{1,3,2,0:T(8,128)(2,1)}, u32[]{:S(2)}, u32[]{:S(2)}) collective-permute-start(bf16[5,320,3,192]{1,3,2,0:T(8,128)(2,1)} %bitcast.199), channel_id=1, source_target_pairs={{0,2},{1,3},{2,0},{3,1},{4,6},{5,7},{6,4},{7,5},{8,10},{9,11},{10,... | collective-permute-start | bytes 5529608 | tf_op jit(solution)/shard_map/ppermute | solution.py:144
  124.3 86.0 %collective-permute-start.2 = (bf16[5,320,3,192]{1,3,2,0:T(8,128)(2,1)}, bf16[5,320,3,192]{1,3,2,0:T(8,128)(2,1)}, u32[]{:S(2)}, u32[]{:S(2)}) collective-permute-start(bf16[5,320,3,192]{1,3,2,0:T(8,128)(2,1)} %bitcast.200), channel_id=1, source_target_pairs={{0,3},{1,2},{2,1},{3,0},{4,7},{5,6},{6,5},{7,4},{8,11},{9,10},{10,... | collective-permute-start | bytes 5529608 | tf_op jit(solution)/shard_map/ppermute | solution.py:144
  210.3 3.4 copy-start.3
  269.3 14.8 copy-start.36
  473.8 11.7 copy-start.33
  473.8 12.3 copy-start.34
  473.8 12.9 copy-start.35
  473.8 13.5 copy-start.23
  481.0 34.1 %all-to-all-start = ((bf16[4,2,153600]{2,1,0:T(2,128)(2,1)}), bf16[4,2,153600]{2,1,0:T(2,128)(2,1)}, u32[]{:S(2)}, u32[]{:S(2)}) async-start(bf16[4,2,153600]{2,1,0:T(2,128)(2,1)} %reshape.451), calls=%async_computation | async-start | bytes 4915200 | tf_op jit(solution)/shard_map/all_to_all | solution.py:148
  488.1 34.3 %copy-start.9 = (f32[5,320]{1,0:T(8,128)}, f32[5,320]{1,0:T(8,128)S(1)}, u32[]{:S(2)}) copy-start(f32[5,320]{1,0:T(8,128)S(1)} %compare_convert_fusion) | copy-start | bytes 19204
  529.4 6.6 copy-start.11
  529.4 6.6 copy-start.32
  542.0 60.1 %copy-start.5 = (f32[1600,768]{1,0:T(8,128)}, f32[1600,768]{1,0:T(8,128)S(1)}, u32[]{:S(2)}) copy-start(f32[1600,768]{1,0:T(8,128)S(1)} %get-tuple-element.292) | copy-start | bytes 14745604
  542.0 0.7 copy-start.29
  542.0 0.8 copy-start.30
  542.0 0.8 copy-start.31
  542.0 60.0 %copy-start.12 = (f32[1600]{0:T(1024)}, f32[1600]{0:T(1024)S(1)}, u32[]{:S(2)}) copy-start(f32[1600]{0:T(1024)S(1)} %broadcast_multiply_fusion.5) | copy-start | bytes 19204
  542.8 59.3 %copy-start.20 = (f32[1600]{0:T(1024)}, f32[1600]{0:T(1024)S(1)}, u32[]{:S(2)}) copy-start(f32[1600]{0:T(1024)S(1)} %add_rsqrt_fusion.1) | copy-start | bytes 19204
  542.8 19.6 %copy-start.8 = (bf16[1600,768]{1,0:T(8,128)(2,1)S(1)}, bf16[1600,768]{1,0:T(8,128)(2,1)}, u32[]{:S(2)}) copy-start(bf16[1600,768]{1,0:T(8,128)(2,1)} %fusion.28) | copy-start | bytes 7372804
  587.0 15.0 copy-start.2
  602.1 5.2 copy-start.38
  607.3 3.6 copy-start.7
  617.3 58.8 %all-to-all-start.1 = ((bf16[5,320,768]{1,0,2:T(8,128)(2,1)}), bf16[5,320,768]{1,0,2:T(8,128)(2,1)}, u32[]{:S(2)}, u32[]{:S(2)}) async-start(bf16[5,320,768]{1,0,2:T(8,128)(2,1)} %copy.82), calls=%async_computation.1 | async-start | bytes 9437184 | tf_op jit(solution)/shard_map/all_to_all | solution.py:190
  676.0 12.4 copy-start.37
  741.4 3.1 copy-start.1
  798.7 3.1 copy-start.1
  855.9 3.1 copy-start.1
  913.2 3.1 copy-start.1
  970.5 3.1 copy-start.1
  994.1 150.1 %all-to-all-start.2 = ((bf16[5,1280,3,192]{3,2,0,1:T(4,128)(2,1)}), bf16[5,1280,3,192]{3,2,0,1:T(4,128)(2,1)}, u32[]{:S(2)}, u32[]{:S(2)}) async-start(bf16[5,1280,3,192]{3,2,0,1:T(4,128)(2,1)} %copy.85), calls=%async_computation.2 | async-start | bytes 26214400 | tf_op jit(solution)/shard_map/all_to_all | solution.py:192
  1000.5 212.1 %reduce-scatter.17.cloned.1.call-start = ((), (), s32[]{:S(2)}) async-start(), calls=%async_computation.12 | async-start | bytes 2654208 | tf_op jit(solution)/shard_map/reduce_scatter | solution.py:212
  1007.2 320.3 %reduce-scatter.15.cloned.1.call-start = ((), (), s32[]{:S(2)}) async-start(), calls=%async_computation.11 | async-start | bytes 7962624 | tf_op jit(solution)/shard_map/reduce_scatter | solution.py:211
  1197.9 294.4 %reduce-scatter.23.cloned.1.call-start = ((), (), s32[]{:S(2)}) async-start(), calls=%async_computation.15 | async-start | bytes 10616832 | tf_op jit(solution)/shard_map/reduce_scatter | solution.py:214
  1212.5 2.1 copy-start.13
  1212.5 2.1 copy-start.21
  1212.5 302.1 %reduce-scatter.27.cloned.1.call-start = ((), (), s32[]{:S(2)}) async-start(), calls=%async_computation.17 | async-start | bytes 491520
  1214.5 465.6 %reduce-scatter.19.cloned.1.call-start = ((), (), s32[]{:S(2)}) async-start(), calls=%async_computation.13 | async-start | bytes 10616832 | tf_op jit(solution)/shard_map/reduce_scatter | solution.py:213
  1230.7 264.4 %copy-start.10 = (f32[5,320]{1,0:T(8,128)S(1)}, f32[5,320]{1,0:T(8,128)}, u32[]{:S(2)}) copy-start(f32[5,320]{1,0:T(8,128)} %copy-done.9) | copy-start | bytes 19204
  1230.7 520.7 %reduce-scatter.25.cloned.1.call-start = ((), (), s32[]{:S(2)}) async-start(), calls=%async_computation.16 | async-start | bytes 1474560
  1330.1 423.1 %reduce-scatter.29.cloned.1.call-start = ((), (), s32[]{:S(2)}) async-start(), calls=%async_computation.18 | async-start | bytes 1474560
  1495.0 269.9 %reduce-scatter.21.cloned.1.call-start = ((), (), s32[]{:S(2)}) async-start(), calls=%async_computation.14 | async-start | bytes 1474560 | tf_op jit(solution)/shard_map/reduce_scatter | solution.py:219
  1498.0 182.2 %copy-start.15 = (f32[768]{0:T(1024)S(1)}, f32[768]{0:T(1024)}, u32[]{:S(2)}) copy-start(f32[768]{0:T(1024)} %copy-done.14) | copy-start | bytes 9220
  1498.0 182.2 %copy-start.17 = (f32[1600]{0:T(1024)S(1)}, f32[1600]{0:T(1024)}, u32[]{:S(2)}) copy-start(f32[1600]{0:T(1024)} %div.27) | copy-start | bytes 19204
  1680.2 14.2 copy-start.19
  1700.8 3.8 copy-start.24
  1700.8 9.2 copy-start.28
Sparse Core Ops, SparseCore 0:
  1007.3 71.1 reduce-scatter.16
  1198.0 129.3 reduce-scatter.14
  1331.1 161.2 reduce-scatter.22
  1494.7 19.9 reduce-scatter.26
  1518.1 162.0 reduce-scatter.18
  1682.6 24.6 reduce-scatter.24
  1710.5 25.6 reduce-scatter.28
  1739.2 25.6 reduce-scatter.20
